TPU v7x, 256 devices: a whole 4x4x8 slice. The times are simulated.
256 devices in a mesh: gx: 32 (over y, z), gy: 8 (over x, core).
Axes of the slice: x: 4, y: 4, z: 8, core: 2. Of those that a mesh axis runs over, the one named last changes fastest.
Arguments:
- densities: bfloat16 [24576, 32, 128], P(('gx', 'gy')), may hold values from -6 to 6
- geometry: float32 [24576, 7, 128], P(('gx', 'gy')), as said below
- near_ids: int32 [24576, 8], P(('gx', 'gy')), may hold values from 0 to 24575, as said below
- basis_in: bfloat16 [24576, 64, 128], P(('gx', 'gy')), may hold values from -0.5 to 0.5
- basis_out: bfloat16 [24576, 64, 128], P(('gx', 'gy')), may hold values from -0.75 to 0.75
- leaf_up: bfloat16 [24576, 64, 64], P(('gx', 'gy')), may hold values from -0.078125 to 0.078125
- leaf_down: bfloat16 [24576, 64, 64], P(('gx', 'gy')), may hold values from -0.75 to 0.75
- leaf_coupling: bfloat16 [24576, 6, 64, 64], P(('gx', 'gy')), may hold values from -0.3125 to 0.3125
- leaf_far: int32 [24576, 6], P(('gx', 'gy')), may hold values from 0 to 24575, as said below
- leaf_count: int32 [24576], P(('gx', 'gy')), may hold values from 1 to 6, as said below
- cluster_up: bfloat16 [256, 64, 64], P(('gx', 'gy')), may hold values from -0.25 to 0.25
- cluster_down: bfloat16 [256, 64, 64], P(('gx', 'gy')), may hold values from -0.75 to 0.75
- cluster_coupling: bfloat16 [256, 6, 64, 64], P(('gx', 'gy')), may hold values from -0.3125 to 0.3125
- cluster_far: int32 [256, 6], P(('gx', 'gy')), may hold values from 0 to 255, as said below
- group_up: bfloat16 [32, 64, 64], replicated, may hold values from -0.375 to 0.375
- group_down: bfloat16 [32, 64, 64], P('gx'), may hold values from -0.75 to 0.75
- group_coupling: bfloat16 [32, 6, 64, 64], P('gx'), may hold values from -0.3125 to 0.3125
- group_far: int32 [32, 6], P('gx'), may hold values from 0 to 31, as said below
- root_coupling: bfloat16 [8, 8, 64, 64], replicated, may hold values from -0.25 to 0.25
Outputs:
- potential: float32 [24576, 32, 128], P(('gx', 'gy'))
Inputs may be any that keep to these rules, and one draw needn't show every extreme that they name: `near_ids`: row l names 8 different leaves of a window of 9 consecutive leaves that contains l, centred on l where the ends allow. `leaf_far`: row l names 6 different leaves held by l's device or its two neighbours in leaf order, none within 4 leaves of l; only the first leaf_count[l] entries are used. `leaf_count`: every device holds a leaf with 6. `cluster_far`: row u names 6 different level-two clusters other than u, of u's group or the two groups beside it. `group_far`: row g names 6 different level-one clusters other than g. `geometry`: rows 0 to 2 hold a panel's centre, rows 3 to 5 its unit normal, row 6 its area, from 0.25 to 2.
All inputs are finite; a program needn't handle non-finite values.
Results may differ from a plain program's by a relative error of at most 0.012.
Values may be sent and summed in bfloat16 or wider, within the bound.
A program may use at most 128 MiB of HBM per device.

v0:
```python
import functools
import math

import jax
import jax.numpy as jnp
from jax import lax
from jax.experimental import pallas as pl
from jax.experimental.pallas import tpu as pltpu
from jax.sharding import PartitionSpec as P

f32 = jnp.float32
bf16 = jnp.bfloat16
MESH = pl.DeviceIdType.MESH
NT = (((1,), (1,)), ((), ()))

REACH = 4
BRANCH = 4
HALO = 8
CHUNK = 8
SPITCH = 65
TPITCH = 33
RPITCH = 97
FAR_LIMIT = 4096.0
VMEM_LIMIT = 67043328


def nt(a, b):
    return lax.dot_general(a, b, NT, preferred_element_type=f32)


def mm(a, b):
    return jnp.dot(a, b, preferred_element_type=f32)


def eye(n):
    rows = lax.broadcasted_iota(jnp.int32, (n, n), 0)
    cols = lax.broadcasted_iota(jnp.int32, (n, n), 1)
    return jnp.where(rows == cols, 1.0, 0.0).astype(bf16)


def split3(x):
    high = x.astype(bf16).astype(f32)
    rest = x - high
    mid = rest.astype(bf16).astype(f32)
    return high, mid, rest - mid


def low_lanes(shape):
    return lax.broadcasted_iota(jnp.int32, shape, len(shape) - 1) < 64


def fold(x):
    return jnp.concatenate([x[:16], x[16:]], axis=1)


def unfold(x):
    return jnp.concatenate([x[:, :64], x[:, 64:]], axis=0)


def slot_of(near_id, first, leaves):
    s = near_id - first
    s = jnp.where(s < 0, s + leaves + HALO, jnp.where(s < leaves, s, s + HALO))
    return jnp.clip(s, 0, leaves + 2 * HALO - 1)


def prepare(geo, rows, base, origin, src, tgt):
    u = [geo[k] - origin[k] for k in range(3)]
    area = geo[6]
    weight = area * (1.0 / (4.0 * math.pi))
    m = [geo[3 + k] * weight for k in range(3)]
    norm = u[0] * u[0] + u[1] * u[1] + u[2] * u[2]
    shift = -(m[0] * u[0] + m[1] * u[1] + m[2] * u[2])
    one = jnp.ones_like(norm)
    zero = jnp.zeros_like(norm)
    us = [split3(x) for x in u]
    vs = [tuple(-2.0 * y for y in x) for x in us]
    ms = [split3(x) for x in m]

    def put(ref, pitch, row, val):
        ref[pl.ds(base * pitch + row, rows, pitch), :] = val

    row = 0
    for k in range(3):
        for i, j in ((0, 0), (0, 1), (1, 0), (0, 2), (2, 0), (1, 1)):
            put(src, SPITCH, row, vs[k][i])
            put(src, SPITCH, 32 + row, ms[k][i])
            if tgt is not None:
                put(tgt, TPITCH, row, us[k][j])
            row += 1
    norms, totals, shifts = split3(norm), split3(norm + area), split3(shift)
    for i in range(3):
        put(src, SPITCH, row, one)
        put(src, SPITCH, 32 + row, zero)
        if tgt is not None:
            put(tgt, TPITCH, row, norms[i])
        row += 1
    for i in range(3):
        put(src, SPITCH, row, totals[i])
        put(src, SPITCH, 32 + row, shifts[i])
        if tgt is not None:
            put(tgt, TPITCH, row, one)
        row += 1
    for r in range(row, 32):
        put(src, SPITCH, r, zero)
        put(src, SPITCH, 32 + r, zero)
        if tgt is not None:
            put(tgt, TPITCH, r, zero)
    return jnp.max(norm)


def up_kernel(
    nx, ny, leaves,
    ids, cluster_far, group_far, geo_hbm, dens_hbm, basis_hbm, up_hbm, down_hbm, cluster_up_hbm, cluster_down_hbm,
    cluster_coupling_hbm, group_up_hbm, group_down_hbm, group_coupling_hbm, root_hbm,
    near_out, lift_out, coeff_out, mid_out, extent_out, dens_halo_out, geo_halo_out,
    geo, dens, basis, up, down, cluster_up, cluster_down, cluster_coupling, group_up, group_down, group_coupling,
    geo_halo, src, tgt, sq, relay, lift, coeff, lhs_all, mid_all, term_all, top_all, root_row, pairs_buf, near,
    in_sem, out_sem, halo_send, halo_recv, coeff_send, coeff_recv, mid_send, mid_recv, term_send, term_recv,
    top_send, top_recv,
):
    gx = lax.axis_index("gx")
    gy = lax.axis_index("gy")
    first = (gx * ny + gy) * leaves
    pairs = leaves // 2
    next_x = lax.rem(gx + 1, nx)
    prev_x = lax.rem(gx + nx - 1, nx)
    right = (jnp.where(gy == ny - 1, next_x, gx), lax.rem(gy + 1, ny))
    left = (jnp.where(gy == 0, prev_x, gx), lax.rem(gy + ny - 1, ny))

    moves = (
        (geo_hbm, geo),
        (down_hbm, down),
        (up_hbm, up),
        (dens_hbm, dens.at[pl.ds(0, leaves)]),
        (basis_hbm, basis),
        (cluster_up_hbm, cluster_up),
        (root_hbm.at[gx // BRANCH], root_row),
        (group_up_hbm, group_up),
        (group_down_hbm, group_down),
        (group_coupling_hbm, group_coupling),
        (cluster_down_hbm, cluster_down),
        (cluster_coupling_hbm, cluster_coupling),
    )
    loads = [pltpu.make_async_copy(a, b, in_sem.at[k]) for k, (a, b) in enumerate(moves)]
    for c in loads:
        c.start()

    barrier = pltpu.get_barrier_semaphore()

    def greet_x(k, c):
        pl.semaphore_signal(barrier, inc=1, device_id=(lax.rem(gx + k, nx), gy), device_id_type=MESH)
        return c

    def greet_y(k, c):
        other = lax.rem(gy + k, ny)
        for x in (prev_x, gx, next_x):
            pl.semaphore_signal(barrier, inc=1, device_id=(x, other), device_id_type=MESH)
        return c

    lax.fori_loop(1, nx, greet_x, 0)
    lax.fori_loop(1, ny, greet_y, 0)

    loads[0].wait()
    origin = [jnp.mean(geo[k, leaves // 2 : leaves // 2 + 1, :], axis=1, keepdims=True) for k in range(3)]
    extent = prepare(geo, leaves, 0, origin, src, tgt)

    ident = eye(leaves)
    loads[1].wait()
    loads[2].wait()

    def relayout(h, c):
        i = 2 * h
        x = jnp.concatenate([down[i], up[i], down[i + 1], up[i + 1]], axis=0)
        y = nt(ident, x)
        relay[pl.ds(i * RPITCH, leaves), :] = y[:, :128]
        relay[pl.ds((i + 1) * RPITCH, leaves), :] = y[:, 128:]
        return c

    lax.fori_loop(0, 32, relayout, 0, unroll=4)

    pl.semaphore_wait(barrier, (nx - 1) + 3 * (ny - 1))
    loads[3].wait()
    halo = []
    for side, (dest, leaf0, row0) in enumerate(
        ((right, leaves - REACH, leaves + HALO - REACH), (left, 0, leaves + HALO))
    ):
        halo.append(
            pltpu.make_async_remote_copy(
                src_ref=dens.at[pl.ds(leaf0, REACH)],
                dst_ref=dens.at[pl.ds(row0, REACH)],
                send_sem=halo_send.at[2 * side],
                recv_sem=halo_recv.at[2 * side],
                device_id=dest,
                device_id_type=MESH,
            )
        )
        halo.append(
            pltpu.make_async_remote_copy(
                src_ref=geo.at[:, pl.ds((leaves - HALO) * (1 - side), HALO), :],
                dst_ref=geo_halo.at[side],
                send_sem=halo_send.at[2 * side + 1],
                recv_sem=halo_recv.at[2 * side + 1],
                device_id=dest,
                device_id_type=MESH,
            )
        )
    for c in halo:
        c.start()

    loads[4].wait()
    low = low_lanes((32, 128))

    def leaf_coeffs(p, c):
        x = dens[pl.ds(2 * p, 2)].reshape(64, 128)
        w = basis[pl.ds(2 * p, 2)].reshape(128, 128)
        y = nt(x, w)
        tile = jnp.where(low, y[:32], y[32:])
        coeff[p] = tile.astype(bf16)
        turned = pltpu.roll(tile, 64, 1)
        lhs_all[p] = jnp.concatenate([jnp.where(low, 0.0, turned), jnp.where(low, 0.0, tile)], axis=1).astype(bf16)
        return c

    def upward(p, acc):
        mats = []
        for b in range(2):
            mat = relay[pl.ds(2 * p + b, 64, RPITCH), :].astype(bf16)
            lift[2 * p + b] = mat
            mats.append(mat)
        return acc + nt(lhs_all[p], jnp.concatenate(mats, axis=1))

    lax.fori_loop(0, pairs, leaf_coeffs, 0, unroll=8)
    mid = lax.fori_loop(0, pairs, upward, jnp.zeros((32, 64), f32), unroll=8)
    loads[5].wait()
    mid = mid.astype(bf16)
    term = nt(mid, cluster_up[0])
    mid_all[ny + gy] = fold(mid.astype(f32)).astype(bf16)
    term_all[gy] = fold(term)

    def term_copy(k):
        other = lax.rem(gy + k, ny)
        return pltpu.make_async_remote_copy(
            src_ref=term_all.at[gy], dst_ref=term_all.at[gy], send_sem=term_send.at[k], recv_sem=term_recv.at[gy],
            device_id=(gx, other), device_id_type=MESH,
        )

    def mid_copy(g, k):
        other = lax.rem(gy + k, ny)
        x = (next_x, gx, prev_x)[g]
        return pltpu.make_async_remote_copy(
            src_ref=mid_all.at[ny + gy], dst_ref=mid_all.at[g * ny + gy], send_sem=mid_send.at[g, k],
            recv_sem=mid_recv.at[g * ny + gy], device_id=(x, other), device_id_type=MESH,
        )

    def top_copy(k):
        return pltpu.make_async_remote_copy(
            src_ref=top_all.at[gx], dst_ref=top_all.at[gx], send_sem=top_send.at[k], recv_sem=top_recv.at[gx],
            device_id=(lax.rem(gx + k, nx), gy), device_id_type=MESH,
        )

    def coeff_copy(side):
        dest = (right, left)[side]
        return pltpu.make_async_remote_copy(
            src_ref=coeff, dst_ref=coeff_out.at[2 * side], send_sem=coeff_send.at[side], recv_sem=coeff_recv.at[side],
            device_id=dest, device_id_type=MESH,
        )

    def start_terms(k, c):
        term_copy(k).start()
        return c

    def start_mids(k, c):
        for g in range(3):
            mid_copy(g, k).start()
        return c

    lax.fori_loop(1, ny, start_terms, 0)
    mid_copy(0, 0).start()
    mid_copy(2, 0).start()
    lax.fori_loop(1, ny, start_mids, 0)

    for c in halo:
        c.wait()
    for side in range(2):
        extent = jnp.maximum(
            extent, prepare(geo_halo.at[side], HALO, leaves + HALO * side, origin, src, None)
        )
    extent_out[...] = jnp.full(extent_out.shape, extent, f32)

    turn = eye(128)

    def transpose(s, c):
        x = src[pl.ds(s * SPITCH, 64), :].astype(bf16)
        sq[s] = nt(turn, x).astype(bf16)
        return c

    lax.fori_loop(0, leaves + 2 * HALO, transpose, 0, unroll=8)
    zero = jnp.zeros((32, 128), bf16)

    def near_chunk(k, c):
        def kernels(b, c):
            l = k * CHUNK + b
            t = tgt[pl.ds(l * TPITCH, 32), :].astype(bf16)
            w = jnp.concatenate([jnp.concatenate([t, zero], 1), jnp.concatenate([zero, t], 1)], 0)
            for n in range(8):
                both = mm(sq[slot_of(ids[n, l], first, leaves)], w)
                f = both[:, 128:]
                r = lax.rsqrt(both[:, :128])
                pairs_buf[b, pl.ds(n * 128, 128), :] = (f * r * (r * r)).astype(bf16)
            return c

        def apply(b, c):
            l = k * CHUNK + b
            values = [dens[slot_of(ids[n, l], first, leaves)] for n in range(8)]
            near[l] = mm(jnp.concatenate(values, 1), pairs_buf[b])
            return c

        lax.fori_loop(0, CHUNK, kernels, 0, unroll=4)
        lax.fori_loop(0, CHUNK, apply, 0, unroll=4)
        return c

    cuts = (0, 3 * CHUNK, 8 * CHUNK, leaves)

    def near_range(a, b):
        lax.fori_loop(a // CHUNK, b // CHUNK, near_chunk, 0)

    near_range(cuts[0], cuts[1])

    def wait_terms(k, c):
        other = lax.rem(gy + k, ny)
        pltpu.make_async_remote_copy(
            src_ref=term_all.at[other], dst_ref=term_all.at[other], send_sem=term_send.at[k],
            recv_sem=term_recv.at[other], device_id=(gx, other), device_id_type=MESH,
        ).wait_recv()
        return c

    lax.fori_loop(1, ny, wait_terms, 0)
    total = term_all[0]
    for u in range(1, ny):
        total = total + term_all[u]
    top_all[gx] = total.astype(bf16)

    def start_tops(k, c):
        top_copy(k).start()
        return c

    lax.fori_loop(1, nx, start_tops, 0)
    for side in range(2):
        coeff_copy(side).start()
    own_coeff = pltpu.make_async_copy(coeff, coeff_out.at[1], out_sem.at[0])
    own_coeff.start()
    lift_copy = pltpu.make_async_copy(lift, lift_out, out_sem.at[1])
    lift_copy.start()
    halo_copy = pltpu.make_async_copy(dens.at[pl.ds(leaves, 2 * HALO)], dens_halo_out, out_sem.at[2])
    halo_copy.start()
    geo_copy = pltpu.make_async_copy(geo_halo, geo_halo_out, out_sem.at[3])
    geo_copy.start()

    near_range(cuts[1], cuts[2])
    near_copies = [
        pltpu.make_async_copy(near.at[pl.ds(0, cuts[2])], near_out.at[pl.ds(0, cuts[2])], out_sem.at[4]),
        pltpu.make_async_copy(
            near.at[pl.ds(cuts[2], leaves - cuts[2])], near_out.at[pl.ds(cuts[2], leaves - cuts[2])], out_sem.at[5]
        ),
    ]
    near_copies[0].start()

    def wait_tops(k, c):
        other = lax.rem(gx + k, nx)
        pltpu.make_async_remote_copy(
            src_ref=top_all.at[other], dst_ref=top_all.at[other], send_sem=top_send.at[k],
            recv_sem=top_recv.at[other], device_id=(other, gy), device_id_type=MESH,
        ).wait_recv()
        return c

    def wait_mid(slot, k):
        pltpu.make_async_remote_copy(
            src_ref=mid_all.at[slot], dst_ref=mid_all.at[slot], send_sem=mid_send.at[0, k],
            recv_sem=mid_recv.at[slot], device_id=(gx, lax.rem(gy + 1, ny)), device_id_type=MESH,
        ).wait_recv()

    def wait_mids(k, c):
        other = lax.rem(gy + k, ny)
        for g in range(3):
            wait_mid(g * ny + other, k)
        return c

    lax.fori_loop(1, nx, wait_tops, 0)
    wait_mid(gy, 0)
    wait_mid(2 * ny + gy, 0)
    lax.fori_loop(1, ny, wait_mids, 0)
    for c in loads[6:]:
        c.wait()

    root_field = jnp.zeros((32, 64), f32)
    for q in range(nx // BRANCH):
        root = jnp.zeros((32, 64), f32)
        for j in range(BRANCH):
            g = q * BRANCH + j
            root = root + nt(unfold(top_all[g]), group_up[g])
        root_field = root_field + nt(root.astype(bf16), root_row[q])
    top_field = nt(root_field.astype(bf16), group_down[0])
    for f in range(group_coupling.shape[1]):
        top_field = top_field + nt(unfold(top_all[group_far[0, f]]), group_coupling[0, f])
    mid_field = nt(top_field.astype(bf16), cluster_down[0])
    for f in range(cluster_coupling.shape[1]):
        u = jnp.clip(cluster_far[0, f] - (gx - 1) * ny, 0, 3 * ny - 1)
        mid_field = mid_field + nt(unfold(mid_all[u]), cluster_coupling[0, f])
    mid_out[...] = jnp.concatenate([mid_field, jnp.zeros((32, 64), f32)], axis=1).astype(bf16)

    near_range(cuts[2], leaves)
    near_copies[1].start()

    def finish_y(k, c):
        term_copy(k).wait_send()
        for g in range(3):
            mid_copy(g, k).wait_send()
        return c

    def finish_x(k, c):
        top_copy(k).wait_send()
        return c

    lax.fori_loop(1, ny, finish_y, 0)
    mid_copy(0, 0).wait_send()
    mid_copy(2, 0).wait_send()
    lax.fori_loop(1, nx, finish_x, 0)
    for side in range(2):
        coeff_copy(side).wait()
    for c in (own_coeff, lift_copy, halo_copy, geo_copy, *near_copies):
        c.wait()


def down_kernel(
    leaves, first_ref, extent, far, count, near_ids, mid, coupling_hbm, lift_hbm, coeff_hbm, near_hbm, basis_hbm,
    geo_hbm, geo_halo_hbm, dens_hbm, dens_halo_hbm,
    out_hbm,
    coupling, lift, pair, dup, near, basis, relay, fields, out, geo, geo_halo, dens, in_sem, out_sem, slow_sem,
):
    first = first_ref[0]
    chunks = 8
    step = 64 // chunks
    pieces = [
        pltpu.make_async_copy(
            coupling_hbm.at[:, pl.ds(k * step, step)], coupling.at[:, pl.ds(k * step, step)], in_sem.at[k]
        )
        for k in range(chunks)
    ]
    coeff_in = pltpu.make_async_copy(coeff_hbm, pair, in_sem.at[chunks])
    others = [
        pltpu.make_async_copy(lift_hbm, lift, in_sem.at[chunks + 1]),
        pltpu.make_async_copy(basis_hbm, basis, in_sem.at[chunks + 2]),
        pltpu.make_async_copy(near_hbm, near, in_sem.at[chunks + 3]),
    ]
    for c in pieces[:4]:
        c.start()
    coeff_in.start()
    for c in pieces[4:]:
        c.start()
    for c in others:
        c.start()

    ident = eye(leaves)
    for k in range(chunks):
        pieces[k].wait()

        def relayout(h, c):
            i = 2 * h
            for f in range(3):
                x = jnp.concatenate(
                    [coupling[2 * f, i], coupling[2 * f + 1, i], coupling[2 * f, i + 1], coupling[2 * f + 1, i + 1]], 0
                )
                y = nt(ident, x)
                relay[f, pl.ds(i * RPITCH, leaves), :] = y[:, :128]
                relay[f, pl.ds((i + 1) * RPITCH, leaves), :] = y[:, 128:]
            return c

        lax.fori_loop(k * step // 2, (k + 1) * step // 2, relayout, 0, unroll=2)

    coeff_in.wait()
    low = low_lanes((32, 128))

    def spread(p, c):
        for side in range(3):
            tile = pair[side, p].astype(f32)
            turned = pltpu.roll(tile, 64, 1)
            dup[side * leaves + 2 * p] = jnp.where(low, tile, turned).astype(bf16)
            dup[side * leaves + 2 * p + 1] = jnp.where(low, turned, tile).astype(bf16)
        return c

    lax.fori_loop(0, leaves // 2, spread, 0, unroll=2)
    dup[3 * leaves] = jnp.zeros((32, 128), bf16)
    for c in others:
        c.wait()

    @pl.when(jnp.logical_not(jnp.max(extent[...]) < FAR_LIMIT))
    def _():
        copies = [
            pltpu.make_async_copy(geo_hbm, geo, slow_sem.at[0]),
            pltpu.make_async_copy(geo_halo_hbm, geo_halo, slow_sem.at[1]),
            pltpu.make_async_copy(dens_hbm, dens.at[pl.ds(0, leaves)], slow_sem.at[2]),
            pltpu.make_async_copy(dens_halo_hbm, dens.at[pl.ds(leaves, 2 * HALO)], slow_sem.at[3]),
        ]
        for c in copies:
            c.start()
        for c in copies:
            c.wait()

        def leaf(l, c):
            near[l] = jnp.zeros((32, 128), f32)

            def one(n, c):
                s = slot_of(near_ids[n, l], first, leaves)
                rows = []
                for k in range(7):
                    local = geo[k, pl.ds(jnp.minimum(s, leaves - 1), 1), :]
                    sl = geo_halo[0, k, pl.ds(jnp.clip(s - leaves, 0, HALO - 1), 1), :]
                    sr = geo_halo[1, k, pl.ds(jnp.clip(s - leaves - HALO, 0, HALO - 1), 1), :]
                    rows.append(jnp.where(s < leaves, local, jnp.where(s < leaves + HALO, sl, sr)))
                rows.append(jnp.zeros((1, 128), f32))
                cols = jnp.concatenate(rows, axis=0).T
                off = [geo[k, pl.ds(l, 1), :] - cols[:, k : k + 1] for k in range(3)]
                area = cols[:, 6:7]
                spread_ = off[0] * off[0] + off[1] * off[1] + off[2] * off[2] + area
                facing = cols[:, 3:4] * off[0] + cols[:, 4:5] * off[1] + cols[:, 5:6] * off[2]
                kern = area * facing / (4.0 * math.pi * spread_ * jnp.sqrt(spread_))
                near[l] += mm(dens[s], kern.astype(bf16))
                return c

            return lax.fori_loop(0, 8, one, c)

        lax.fori_loop(0, leaves, leaf, 0)

    parent = mid[...]

    def leaf(l, c):
        lhs, mats = [], []
        for f in range(3):
            tiles = []
            for b in range(2):
                k = 2 * f + b
                s = jnp.where(k < count[l], far[k, l] - (first - leaves), 3 * leaves)
                s = jnp.clip(s, 0, 3 * leaves)
                tiles.append(dup[s])
            lhs.append(jnp.where(low, tiles[0], tiles[1]))
            mats.append(relay[f, pl.ds(l, 64, RPITCH), :].astype(bf16))
        lhs.append(parent)
        mats.append(lift[l])
        fields[l] = nt(jnp.concatenate(lhs, 1), jnp.concatenate(mats, 1)).astype(bf16)
        return c

    def panels(l, c):
        out[l] = mm(fields[l], basis[l]) + near[l]
        return c

    parts = 4
    size = leaves // parts
    stores = []
    for k in range(parts):
        lax.fori_loop(k * size, (k + 1) * size, leaf, 0, unroll=8)
        lax.fori_loop(k * size, (k + 1) * size, panels, 0, unroll=8)
        stores.append(
            pltpu.make_async_copy(out.at[pl.ds(k * size, size)], out_hbm.at[pl.ds(k * size, size)], out_sem.at[k])
        )
        stores[-1].start()
    for c in stores:
        c.wait()


def down_call(leaves, *args):
    V = pl.BlockSpec(memory_space=pltpu.VMEM)
    S = pl.BlockSpec(memory_space=pltpu.SMEM)
    H = pl.BlockSpec(memory_space=pl.ANY)
    dma = pltpu.SemaphoreType.DMA
    shape = jax.ShapeDtypeStruct
    slots = leaves + 2 * HALO
    return pl.pallas_call(
        functools.partial(down_kernel, leaves),
        name="down",
        out_shape=shape((leaves, 32, 128), f32),
        in_specs=[S, V, S, S, S, V] + [H] * 9,
        out_specs=H,
        scratch_shapes=[
            pltpu.VMEM((6, 64, 64, leaves), bf16),
            pltpu.VMEM((leaves, 64, 128), bf16),
            pltpu.VMEM((3, leaves // 2, 32, 128), bf16),
            pltpu.VMEM((3 * leaves + 1, 32, 128), bf16),
            pltpu.VMEM((leaves, 32, 128), f32),
            pltpu.VMEM((leaves, 64, 128), bf16),
            pltpu.VMEM((3, 64 * RPITCH, 128), f32),
            pltpu.VMEM((leaves, 32, 64), bf16),
            pltpu.VMEM((leaves, 32, 128), f32),
            pltpu.VMEM((7, leaves, 128), f32),
            pltpu.VMEM((2, 7, HALO, 128), f32),
            pltpu.VMEM((slots, 32, 128), bf16),
            dma((12,)), dma((4,)), dma((4,)),
        ],
        compiler_params=pltpu.CompilerParams(vmem_limit_bytes=VMEM_LIMIT),
    )(*args)


def on_device(
    nx, ny, densities, geometry, near_ids, basis_in, basis_out, leaf_up, leaf_down, leaf_coupling, leaf_far, leaf_count,
    cluster_up, cluster_down, cluster_coupling, cluster_far, group_up, group_down, group_coupling, group_far,
    root_coupling,
):
    leaves = densities.shape[0]
    slots = leaves + 2 * HALO
    geo = jnp.transpose(geometry, (1, 0, 2))
    up = jnp.transpose(leaf_up, (1, 2, 0))
    down = jnp.transpose(leaf_down, (1, 2, 0))
    coupling = jnp.transpose(leaf_coupling, (1, 2, 3, 0))
    ids = near_ids.T
    far = leaf_far.T
    V = pl.BlockSpec(memory_space=pltpu.VMEM)
    S = pl.BlockSpec(memory_space=pltpu.SMEM)
    H = pl.BlockSpec(memory_space=pl.ANY)
    dma = pltpu.SemaphoreType.DMA
    shape = jax.ShapeDtypeStruct
    near, lift, coeff, mid, extent, dens_halo, geo_halo = pl.pallas_call(
        functools.partial(up_kernel, nx, ny, leaves),
        name="up",
        out_shape=(
            shape((leaves, 32, 128), f32),
            shape((leaves, 64, 128), bf16),
            shape((3, leaves // 2, 32, 128), bf16),
            shape((32, 128), bf16),
            shape((8, 128), f32),
            shape((2 * HALO, 32, 128), bf16),
            shape((2, 7, HALO, 128), f32),
        ),
        in_specs=[S, S, S] + [H] * 12,
        out_specs=(H, H, H, V, V, H, H),
        scratch_shapes=[
            pltpu.VMEM((7, leaves, 128), f32),
            pltpu.VMEM((slots, 32, 128), bf16),
            pltpu.VMEM((leaves, 64, 128), bf16),
            pltpu.VMEM((64, 64, leaves), bf16),
            pltpu.VMEM((64, 64, leaves), bf16),
            pltpu.VMEM((1, 64, 64), bf16),
            pltpu.VMEM((1, 64, 64), bf16),
            pltpu.VMEM(cluster_coupling.shape, bf16),
            pltpu.VMEM(group_up.shape, bf16),
            pltpu.VMEM((1, 64, 64), bf16),
            pltpu.VMEM(group_coupling.shape, bf16),
            pltpu.VMEM((2, 7, HALO, 128), f32),
            pltpu.VMEM((slots * SPITCH, 128), f32),
            pltpu.VMEM((leaves * TPITCH, 128), f32),
            pltpu.VMEM((slots, 128, 64), bf16),
            pltpu.VMEM((64 * RPITCH, 128), f32),
            pltpu.VMEM((leaves, 64, 128), bf16),
            pltpu.VMEM((leaves // 2, 32, 128), bf16),
            pltpu.VMEM((leaves // 2, 32, 256), bf16),
            pltpu.VMEM((3 * ny, 16, 128), bf16),
            pltpu.VMEM((ny, 16, 128), f32),
            pltpu.VMEM((nx, 16, 128), bf16),
            pltpu.VMEM((nx // BRANCH, 64, 64), bf16),
            pltpu.VMEM((CHUNK, 8 * 128, 128), bf16),
            pltpu.VMEM((leaves, 32, 128), f32),
            dma((12,)), dma((6,)), dma((4,)), dma((4,)), dma((2,)), dma((2,)), dma((3, ny)), dma((3 * ny,)),
            dma((ny,)), dma((ny,)), dma((nx,)), dma((nx,)),
        ],
        compiler_params=pltpu.CompilerParams(
            collective_id=0, has_side_effects=True, vmem_limit_bytes=VMEM_LIMIT
        ),
    )(
        ids, cluster_far, group_far, geo, densities, basis_in, up, down, cluster_up, cluster_down, cluster_coupling,
        group_up, group_down, group_coupling, root_coupling,
    )
    first = ((lax.axis_index("gx") * ny + lax.axis_index("gy")) * leaves).reshape(1)
    return down_call(
        leaves, first, extent, far, leaf_count, ids, mid, coupling, lift, coeff, near, basis_out, geo, geo_halo,
        densities, dens_halo,
    )


def solution(mesh):
    leaf = ("gx", "gy")
    return jax.shard_map(
        functools.partial(on_device, mesh.shape["gx"], mesh.shape["gy"]),
        mesh=mesh,
        in_specs=(
            P(leaf, None, None),
            P(leaf, None, None),
            P(leaf, None),
            P(leaf, None, None),
            P(leaf, None, None),
            P(leaf, None, None),
            P(leaf, None, None),
            P(leaf, None, None, None),
            P(leaf, None),
            P(leaf),
            P(leaf, None, None),
            P(leaf, None, None),
            P(leaf, None, None, None),
            P(leaf, None),
            P(),
            P("gx", None, None),
            P("gx", None, None, None),
            P("gx", None),
            P(),
        ),
        out_specs=P(leaf, None, None),
        check_vma=False,
    )
```

profile of v0, /device:TPU:1, one launch (start us, length us, event | category | flops | bytes accessed | tf_op | source)
XLA Modules:
  0.0 64.7 jit_solution(4839183100572226167)
XLA Ops:
  0.0 49.7 %up.1 = (f32[96,32,128]{2,1,0:T(8,128)}, bf16[96,64,128]{2,1,0:T(8,128)(2,1)}, bf16[3,48,32,128]{3,2,1,0:T(8,128)(2,1)}, bf16[32,128]{1,0:T(8,128)(2,1)}, f32[8,...) custom-call(s32[8,96]{1,0:T(8,128)} %bitcast.12, s32[1,6]{1,0:T(1,128)} %cluster_far.1, ...), custom_call_target="tpu_custom_call" | custom-call | tf_op jit(solution)/shard_map/up/pallas_call | solution.py:619
  49.7 15.0 %down.1 = f32[96,32,128]{2,1,0:T(8,128)} custom-call(s32[1]{0:T(128)} %bitcast.first_ref, f32[8,128]{1,0:T(8,128)} %get-tuple-element.12.extent, s32[6,96]{1,0:T(8,128)} %bitcast.14, s32[96]{0:T(128)} %count.1, s32[8,96]{1,0:T(8,128)} %bitcast.13, bf16[32,128]{1,0:T(8,128)(2,1)} %get-tuple-element.13.mid, bf16[6,64,64,96]{3,2,1,0:T(8,128)(2,1)} %bitcast.7, ...), custom_call_target="tpu_custom_call" | custom-call | tf_op jit(solution)/shard_map/down/pallas_call | solution.py:576
where the time goes:
time: 64.8 us; the launch traced here: 64.7 us
  Pallas kernels  64.7 us (100%)
    pallas_call x1, Pallas kernels, on_device(): pl.pallas_call(functools.partial(up_kernel, nx, ny, leaves), name='up', o...  49.7 us
    pallas_call x1, Pallas kernels, down_call(): pl.pallas_call(functools.partial(down_kernel, leaves), name='down', out_s...  15 us

commit v1 on v0

--- a/solution.py
+++ b/solution.py
@@ -110,11 +110,12 @@
 
 def up_kernel(
     nx, ny, leaves,
-    ids, cluster_far, group_far, geo_hbm, dens_hbm, basis_hbm, up_hbm, down_hbm, cluster_up_hbm, cluster_down_hbm,
+    ids, far, count, cluster_far, group_far, geo_hbm, dens_hbm, basis_hbm, up_hbm, down_hbm, cluster_up_hbm, cluster_down_hbm,
     cluster_coupling_hbm, group_up_hbm, group_down_hbm, group_coupling_hbm, root_hbm,
-    near_out, lift_out, coeff_out, mid_out, extent_out, dens_halo_out, geo_halo_out,
-    geo, dens, basis, up, down, cluster_up, cluster_down, cluster_coupling, group_up, group_down, group_coupling,
-    geo_halo, src, tgt, sq, relay, lift, coeff, lhs_all, mid_all, term_all, top_all, root_row, pairs_buf, near,
+    coupling_hbm, panel_basis_hbm,
+    total_out, field_out, extent_out, dens_halo_out, geo_halo_out,
+    geo, dens, basis, panel_basis, up, down, cluster_up, cluster_down, cluster_coupling, group_up, group_down, group_coupling,
+    geo_halo, dens_halo, src, tgt, sq, relay, coupling, coupling_relay, lift, coeff, dup, field, lhs_all, mid_all, term_all, top_all, root_row, pairs_buf, near,
     in_sem, out_sem, halo_send, halo_recv, coeff_send, coeff_recv, mid_send, mid_recv, term_send, term_recv,
     top_send, top_recv,
 ):
@@ -140,6 +141,8 @@
         (group_coupling_hbm, group_coupling),
         (cluster_down_hbm, cluster_down),
         (cluster_coupling_hbm, cluster_coupling),
+        (coupling_hbm, coupling),
+        (panel_basis_hbm, panel_basis),
     )
     loads = [pltpu.make_async_copy(a, b, in_sem.at[k]) for k, (a, b) in enumerate(moves)]
     for c in loads:
@@ -176,18 +179,62 @@
         relay[pl.ds((i + 1) * RPITCH, leaves), :] = y[:, 128:]
         return c
 
-    lax.fori_loop(0, 32, relayout, 0, unroll=4)
+    lax.fori_loop(0, 32, relayout, 0, unroll=8)
+
+    loads[3].wait()
+    loads[4].wait()
+    low = low_lanes((32, 128))
+
+    def leaf_coeffs(p, c):
+        x = dens[pl.ds(2 * p, 2)].reshape(64, 128)
+        w = basis[pl.ds(2 * p, 2)].reshape(128, 128)
+        y = nt(x, w)
+        tile = jnp.where(low, y[:32], y[32:])
+        coeff[1, p] = tile.astype(bf16)
+        turned = pltpu.roll(tile, 64, 1)
+        lhs_all[p] = jnp.concatenate([jnp.where(low, 0.0, turned), jnp.where(low, 0.0, tile)], axis=1).astype(bf16)
+        return c
+
+    def upward(p, acc):
+        mats = []
+        for b in range(2):
+            mat = relay[pl.ds(2 * p + b, 64, RPITCH), :].astype(bf16)
+            lift[2 * p + b] = mat
+            mats.append(mat)
+        return acc + nt(lhs_all[p], jnp.concatenate(mats, axis=1))
+
+    lax.fori_loop(0, pairs, leaf_coeffs, 0, unroll=8)
+    mid = lax.fori_loop(0, pairs, upward, jnp.zeros((32, 64), f32), unroll=16)
+    loads[5].wait()
+    mid = mid.astype(bf16)
+    term = nt(mid, cluster_up[0])
+    mid_all[ny + gy] = fold(mid.astype(f32)).astype(bf16)
+    term_all[gy] = fold(term)
+
+    loads[12].wait()
+
+    def relayout_coupling(h, c):
+        i = 2 * h
+        for f in range(3):
+            x = jnp.concatenate(
+                [coupling[2 * f, i], coupling[2 * f + 1, i], coupling[2 * f, i + 1], coupling[2 * f + 1, i + 1]], 0
+            )
+            y = nt(ident, x)
+            coupling_relay[f, pl.ds(i * RPITCH, leaves), :] = y[:, :128]
+            coupling_relay[f, pl.ds((i + 1) * RPITCH, leaves), :] = y[:, 128:]
+        return c
+
+    lax.fori_loop(0, 32, relayout_coupling, 0, unroll=8)
 
     pl.semaphore_wait(barrier, (nx - 1) + 3 * (ny - 1))
-    loads[3].wait()
     halo = []
     for side, (dest, leaf0, row0) in enumerate(
-        ((right, leaves - REACH, leaves + HALO - REACH), (left, 0, leaves + HALO))
+        ((right, leaves - REACH, HALO - REACH), (left, 0, HALO))
     ):
         halo.append(
             pltpu.make_async_remote_copy(
                 src_ref=dens.at[pl.ds(leaf0, REACH)],
-                dst_ref=dens.at[pl.ds(row0, REACH)],
+                dst_ref=dens_halo.at[pl.ds(row0, REACH)],
                 send_sem=halo_send.at[2 * side],
                 recv_sem=halo_recv.at[2 * side],
                 device_id=dest,
@@ -204,37 +251,6 @@
                 device_id_type=MESH,
             )
         )
-    for c in halo:
-        c.start()
-
-    loads[4].wait()
-    low = low_lanes((32, 128))
-
-    def leaf_coeffs(p, c):
-        x = dens[pl.ds(2 * p, 2)].reshape(64, 128)
-        w = basis[pl.ds(2 * p, 2)].reshape(128, 128)
-        y = nt(x, w)
-        tile = jnp.where(low, y[:32], y[32:])
-        coeff[p] = tile.astype(bf16)
-        turned = pltpu.roll(tile, 64, 1)
-        lhs_all[p] = jnp.concatenate([jnp.where(low, 0.0, turned), jnp.where(low, 0.0, tile)], axis=1).astype(bf16)
-        return c
-
-    def upward(p, acc):
-        mats = []
-        for b in range(2):
-            mat = relay[pl.ds(2 * p + b, 64, RPITCH), :].astype(bf16)
-            lift[2 * p + b] = mat
-            mats.append(mat)
-        return acc + nt(lhs_all[p], jnp.concatenate(mats, axis=1))
-
-    lax.fori_loop(0, pairs, leaf_coeffs, 0, unroll=8)
-    mid = lax.fori_loop(0, pairs, upward, jnp.zeros((32, 64), f32), unroll=8)
-    loads[5].wait()
-    mid = mid.astype(bf16)
-    term = nt(mid, cluster_up[0])
-    mid_all[ny + gy] = fold(mid.astype(f32)).astype(bf16)
-    term_all[gy] = fold(term)
 
     def term_copy(k):
         other = lax.rem(gy + k, ny)
@@ -260,7 +276,7 @@
     def coeff_copy(side):
         dest = (right, left)[side]
         return pltpu.make_async_remote_copy(
-            src_ref=coeff, dst_ref=coeff_out.at[2 * side], send_sem=coeff_send.at[side], recv_sem=coeff_recv.at[side],
+            src_ref=coeff.at[1], dst_ref=coeff.at[2 * side], send_sem=coeff_send.at[side], recv_sem=coeff_recv.at[side],
             device_id=dest, device_id_type=MESH,
         )
 
@@ -274,18 +290,12 @@
         return c
 
     lax.fori_loop(1, ny, start_terms, 0)
+    for c in halo:
+        c.start()
     mid_copy(0, 0).start()
     mid_copy(2, 0).start()
     lax.fori_loop(1, ny, start_mids, 0)
 
-    for c in halo:
-        c.wait()
-    for side in range(2):
-        extent = jnp.maximum(
-            extent, prepare(geo_halo.at[side], HALO, leaves + HALO * side, origin, src, None)
-        )
-    extent_out[...] = jnp.full(extent_out.shape, extent, f32)
-
     turn = eye(128)
 
     def transpose(s, c):
@@ -293,7 +303,7 @@
         sq[s] = nt(turn, x).astype(bf16)
         return c
 
-    lax.fori_loop(0, leaves + 2 * HALO, transpose, 0, unroll=8)
+    lax.fori_loop(0, leaves, transpose, 0, unroll=16)
     zero = jnp.zeros((32, 128), bf16)
 
     def near_chunk(k, c):
@@ -314,14 +324,15 @@
             near[l] = mm(jnp.concatenate(values, 1), pairs_buf[b])
             return c
 
-        lax.fori_loop(0, CHUNK, kernels, 0, unroll=4)
-        lax.fori_loop(0, CHUNK, apply, 0, unroll=4)
-        return c
-
-    cuts = (0, 3 * CHUNK, 8 * CHUNK, leaves)
+        lax.fori_loop(0, CHUNK, kernels, 0, unroll=8)
+        lax.fori_loop(0, CHUNK, apply, 0, unroll=8)
+        return c
+
+    chunks = leaves // CHUNK
+    cuts = (1, 3, 9, chunks - 1)
 
     def near_range(a, b):
-        lax.fori_loop(a // CHUNK, b // CHUNK, near_chunk, 0)
+        lax.fori_loop(a, b, near_chunk, 0)
 
     near_range(cuts[0], cuts[1])
 
@@ -346,24 +357,7 @@
     lax.fori_loop(1, nx, start_tops, 0)
     for side in range(2):
         coeff_copy(side).start()
-    own_coeff = pltpu.make_async_copy(coeff, coeff_out.at[1], out_sem.at[0])
-    own_coeff.start()
-    lift_copy = pltpu.make_async_copy(lift, lift_out, out_sem.at[1])
-    lift_copy.start()
-    halo_copy = pltpu.make_async_copy(dens.at[pl.ds(leaves, 2 * HALO)], dens_halo_out, out_sem.at[2])
-    halo_copy.start()
-    geo_copy = pltpu.make_async_copy(geo_halo, geo_halo_out, out_sem.at[3])
-    geo_copy.start()
-
     near_range(cuts[1], cuts[2])
-    near_copies = [
-        pltpu.make_async_copy(near.at[pl.ds(0, cuts[2])], near_out.at[pl.ds(0, cuts[2])], out_sem.at[4]),
-        pltpu.make_async_copy(
-            near.at[pl.ds(cuts[2], leaves - cuts[2])], near_out.at[pl.ds(cuts[2], leaves - cuts[2])], out_sem.at[5]
-        ),
-    ]
-    near_copies[0].start()
-
     def wait_tops(k, c):
         other = lax.rem(gx + k, nx)
         pltpu.make_async_remote_copy(
@@ -388,7 +382,7 @@
     wait_mid(gy, 0)
     wait_mid(2 * ny + gy, 0)
     lax.fori_loop(1, ny, wait_mids, 0)
-    for c in loads[6:]:
+    for c in loads[6:12]:
         c.wait()
 
     root_field = jnp.zeros((32, 64), f32)
@@ -405,10 +399,70 @@
     for f in range(cluster_coupling.shape[1]):
         u = jnp.clip(cluster_far[0, f] - (gx - 1) * ny, 0, 3 * ny - 1)
         mid_field = mid_field + nt(unfold(mid_all[u]), cluster_coupling[0, f])
-    mid_out[...] = jnp.concatenate([mid_field, jnp.zeros((32, 64), f32)], axis=1).astype(bf16)
-
-    near_range(cuts[2], leaves)
-    near_copies[1].start()
+    parent = jnp.concatenate([mid_field, jnp.zeros((32, 64), f32)], axis=1).astype(bf16)
+
+    near_range(cuts[2], cuts[3])
+    for c in halo:
+        c.wait()
+    dens[pl.ds(leaves + HALO - REACH, 2 * REACH)] = dens_halo[pl.ds(HALO - REACH, 2 * REACH)]
+    for side in range(2):
+        extent = jnp.maximum(
+            extent, prepare(geo_halo.at[side], HALO, leaves + HALO * side, origin, src, None)
+        )
+    extent_out[...] = jnp.full(extent_out.shape, extent, f32)
+
+    halo_copy = pltpu.make_async_copy(dens_halo, dens_halo_out, out_sem.at[0])
+    halo_copy.start()
+    geo_copy = pltpu.make_async_copy(geo_halo, geo_halo_out, out_sem.at[1])
+    geo_copy.start()
+
+    lax.fori_loop(leaves, leaves + 2 * HALO, transpose, 0, unroll=16)
+    lax.fori_loop(0, 2, lambda k, c: near_chunk(k * (chunks - 1), c), 0)
+
+    for side in range(2):
+        coeff_copy(side).wait()
+
+    def spread(p, c):
+        for side in range(3):
+            tile = coeff[side, p].astype(f32)
+            turned = pltpu.roll(tile, 64, 1)
+            dup[side * leaves + 2 * p] = jnp.where(low, tile, turned).astype(bf16)
+            dup[side * leaves + 2 * p + 1] = jnp.where(low, turned, tile).astype(bf16)
+        return c
+
+    lax.fori_loop(0, pairs, spread, 0, unroll=8)
+    dup[3 * leaves] = jnp.zeros((32, 128), bf16)
+
+    def leaf_fields(l, c):
+        lhs, mats = [], []
+        for f in range(3):
+            tiles = []
+            for b in range(2):
+                k = 2 * f + b
+                s = jnp.where(k < count[l], far[k, l] - (first - leaves), 3 * leaves)
+                tiles.append(dup[jnp.clip(s, 0, 3 * leaves)])
+            lhs.append(jnp.where(low, tiles[0], tiles[1]))
+            mats.append(coupling_relay[f, pl.ds(l, 64, RPITCH), :].astype(bf16))
+        lhs.append(parent)
+        mats.append(lift[l])
+        field[l] = nt(jnp.concatenate(lhs, 1), jnp.concatenate(mats, 1)).astype(bf16)
+        return c
+
+    def panels(l, c):
+        near[l] = near[l] + mm(field[l], panel_basis[l])
+        return c
+
+    lax.fori_loop(0, leaves, leaf_fields, 0, unroll=16)
+    field_copy = pltpu.make_async_copy(field, field_out, out_sem.at[2])
+    field_copy.start()
+    loads[13].wait()
+    third = leaves // 3
+    total_copies = []
+    for k in range(3):
+        lax.fori_loop(k * third, (k + 1) * third, panels, 0, unroll=8)
+        rows = pl.ds(k * third, third)
+        total_copies.append(pltpu.make_async_copy(near.at[rows], total_out.at[rows], out_sem.at[3 + k]))
+        total_copies[-1].start()
 
     def finish_y(k, c):
         term_copy(k).wait_send()
@@ -424,81 +478,44 @@
     mid_copy(0, 0).wait_send()
     mid_copy(2, 0).wait_send()
     lax.fori_loop(1, nx, finish_x, 0)
-    for side in range(2):
-        coeff_copy(side).wait()
-    for c in (own_coeff, lift_copy, halo_copy, geo_copy, *near_copies):
+    for c in (halo_copy, geo_copy, field_copy, *total_copies):
         c.wait()
 
 
-def down_kernel(
-    leaves, first_ref, extent, far, count, near_ids, mid, coupling_hbm, lift_hbm, coeff_hbm, near_hbm, basis_hbm,
-    geo_hbm, geo_halo_hbm, dens_hbm, dens_halo_hbm,
+def finish_kernel(
+    leaves, first_ref, extent, near_ids, total_hbm, field_hbm, basis_hbm, geo_hbm, geo_halo_hbm, dens_hbm, dens_halo_hbm,
     out_hbm,
-    coupling, lift, pair, dup, near, basis, relay, fields, out, geo, geo_halo, dens, in_sem, out_sem, slow_sem,
+    out, field, basis, geo, geo_halo, dens, in_sem, out_sem, slow_sem,
 ):
     first = first_ref[0]
-    chunks = 8
-    step = 64 // chunks
-    pieces = [
-        pltpu.make_async_copy(
-            coupling_hbm.at[:, pl.ds(k * step, step)], coupling.at[:, pl.ds(k * step, step)], in_sem.at[k]
-        )
-        for k in range(chunks)
-    ]
-    coeff_in = pltpu.make_async_copy(coeff_hbm, pair, in_sem.at[chunks])
-    others = [
-        pltpu.make_async_copy(lift_hbm, lift, in_sem.at[chunks + 1]),
-        pltpu.make_async_copy(basis_hbm, basis, in_sem.at[chunks + 2]),
-        pltpu.make_async_copy(near_hbm, near, in_sem.at[chunks + 3]),
-    ]
-    for c in pieces[:4]:
+    parts = 4
+    size = leaves // parts
+    rows = [pl.ds(k * size, size) for k in range(parts)]
+    ins = [pltpu.make_async_copy(total_hbm.at[r], out.at[r], in_sem.at[k]) for k, r in enumerate(rows)]
+    outs = [pltpu.make_async_copy(out.at[r], out_hbm.at[r], out_sem.at[k]) for k, r in enumerate(rows)]
+    for c in ins:
         c.start()
-    coeff_in.start()
-    for c in pieces[4:]:
-        c.start()
-    for c in others:
-        c.start()
-
-    ident = eye(leaves)
-    for k in range(chunks):
-        pieces[k].wait()
-
-        def relayout(h, c):
-            i = 2 * h
-            for f in range(3):
-                x = jnp.concatenate(
-                    [coupling[2 * f, i], coupling[2 * f + 1, i], coupling[2 * f, i + 1], coupling[2 * f + 1, i + 1]], 0
-                )
-                y = nt(ident, x)
-                relay[f, pl.ds(i * RPITCH, leaves), :] = y[:, :128]
-                relay[f, pl.ds((i + 1) * RPITCH, leaves), :] = y[:, 128:]
-            return c
-
-        lax.fori_loop(k * step // 2, (k + 1) * step // 2, relayout, 0, unroll=2)
-
-    coeff_in.wait()
-    low = low_lanes((32, 128))
-
-    def spread(p, c):
-        for side in range(3):
-            tile = pair[side, p].astype(f32)
-            turned = pltpu.roll(tile, 64, 1)
-            dup[side * leaves + 2 * p] = jnp.where(low, tile, turned).astype(bf16)
-            dup[side * leaves + 2 * p + 1] = jnp.where(low, turned, tile).astype(bf16)
-        return c
-
-    lax.fori_loop(0, leaves // 2, spread, 0, unroll=2)
-    dup[3 * leaves] = jnp.zeros((32, 128), bf16)
-    for c in others:
-        c.wait()
-
-    @pl.when(jnp.logical_not(jnp.max(extent[...]) < FAR_LIMIT))
+    resolved = jnp.max(extent[...]) < FAR_LIMIT
+
+    @pl.when(resolved)
     def _():
+        for i, o in zip(ins, outs):
+            i.wait()
+            o.start()
+        for o in outs:
+            o.wait()
+
+    @pl.when(jnp.logical_not(resolved))
+    def _():
+        for i in ins:
+            i.wait()
         copies = [
             pltpu.make_async_copy(geo_hbm, geo, slow_sem.at[0]),
             pltpu.make_async_copy(geo_halo_hbm, geo_halo, slow_sem.at[1]),
             pltpu.make_async_copy(dens_hbm, dens.at[pl.ds(0, leaves)], slow_sem.at[2]),
             pltpu.make_async_copy(dens_halo_hbm, dens.at[pl.ds(leaves, 2 * HALO)], slow_sem.at[3]),
+            pltpu.make_async_copy(field_hbm, field, slow_sem.at[4]),
+            pltpu.make_async_copy(basis_hbm, basis, slow_sem.at[5]),
         ]
         for c in copies:
             c.start()
@@ -506,7 +523,7 @@
             c.wait()
 
         def leaf(l, c):
-            near[l] = jnp.zeros((32, 128), f32)
+            out[l] = mm(field[l], basis[l])
 
             def one(n, c):
                 s = slot_of(near_ids[n, l], first, leaves)
@@ -520,82 +537,19 @@
                 cols = jnp.concatenate(rows, axis=0).T
                 off = [geo[k, pl.ds(l, 1), :] - cols[:, k : k + 1] for k in range(3)]
                 area = cols[:, 6:7]
-                spread_ = off[0] * off[0] + off[1] * off[1] + off[2] * off[2] + area
+                wide = off[0] * off[0] + off[1] * off[1] + off[2] * off[2] + area
                 facing = cols[:, 3:4] * off[0] + cols[:, 4:5] * off[1] + cols[:, 5:6] * off[2]
-                kern = area * facing / (4.0 * math.pi * spread_ * jnp.sqrt(spread_))
-                near[l] += mm(dens[s], kern.astype(bf16))
+                kern = area * facing / (4.0 * math.pi * wide * jnp.sqrt(wide))
+                out[l] += mm(dens[s], kern.astype(bf16))
                 return c
 
             return lax.fori_loop(0, 8, one, c)
 
         lax.fori_loop(0, leaves, leaf, 0)
-
-    parent = mid[...]
-
-    def leaf(l, c):
-        lhs, mats = [], []
-        for f in range(3):
-            tiles = []
-            for b in range(2):
-                k = 2 * f + b
-                s = jnp.where(k < count[l], far[k, l] - (first - leaves), 3 * leaves)
-                s = jnp.clip(s, 0, 3 * leaves)
-                tiles.append(dup[s])
-            lhs.append(jnp.where(low, tiles[0], tiles[1]))
-            mats.append(relay[f, pl.ds(l, 64, RPITCH), :].astype(bf16))
-        lhs.append(parent)
-        mats.append(lift[l])
-        fields[l] = nt(jnp.concatenate(lhs, 1), jnp.concatenate(mats, 1)).astype(bf16)
-        return c
-
-    def panels(l, c):
-        out[l] = mm(fields[l], basis[l]) + near[l]
-        return c
-
-    parts = 4
-    size = leaves // parts
-    stores = []
-    for k in range(parts):
-        lax.fori_loop(k * size, (k + 1) * size, leaf, 0, unroll=8)
-        lax.fori_loop(k * size, (k + 1) * size, panels, 0, unroll=8)
-        stores.append(
-            pltpu.make_async_copy(out.at[pl.ds(k * size, size)], out_hbm.at[pl.ds(k * size, size)], out_sem.at[k])
-        )
-        stores[-1].start()
-    for c in stores:
-        c.wait()
-
-
-def down_call(leaves, *args):
-    V = pl.BlockSpec(memory_space=pltpu.VMEM)
-    S = pl.BlockSpec(memory_space=pltpu.SMEM)
-    H = pl.BlockSpec(memory_space=pl.ANY)
-    dma = pltpu.SemaphoreType.DMA
-    shape = jax.ShapeDtypeStruct
-    slots = leaves + 2 * HALO
-    return pl.pallas_call(
-        functools.partial(down_kernel, leaves),
-        name="down",
-        out_shape=shape((leaves, 32, 128), f32),
-        in_specs=[S, V, S, S, S, V] + [H] * 9,
-        out_specs=H,
-        scratch_shapes=[
-            pltpu.VMEM((6, 64, 64, leaves), bf16),
-            pltpu.VMEM((leaves, 64, 128), bf16),
-            pltpu.VMEM((3, leaves // 2, 32, 128), bf16),
-            pltpu.VMEM((3 * leaves + 1, 32, 128), bf16),
-            pltpu.VMEM((leaves, 32, 128), f32),
-            pltpu.VMEM((leaves, 64, 128), bf16),
-            pltpu.VMEM((3, 64 * RPITCH, 128), f32),
-            pltpu.VMEM((leaves, 32, 64), bf16),
-            pltpu.VMEM((leaves, 32, 128), f32),
-            pltpu.VMEM((7, leaves, 128), f32),
-            pltpu.VMEM((2, 7, HALO, 128), f32),
-            pltpu.VMEM((slots, 32, 128), bf16),
-            dma((12,)), dma((4,)), dma((4,)),
-        ],
-        compiler_params=pltpu.CompilerParams(vmem_limit_bytes=VMEM_LIMIT),
-    )(*args)
+        for o in outs:
+            o.start()
+        for o in outs:
+            o.wait()
 
 
 def on_device(
@@ -616,23 +570,22 @@
     H = pl.BlockSpec(memory_space=pl.ANY)
     dma = pltpu.SemaphoreType.DMA
     shape = jax.ShapeDtypeStruct
-    near, lift, coeff, mid, extent, dens_halo, geo_halo = pl.pallas_call(
+    total, field, extent, dens_halo, geo_halo = pl.pallas_call(
         functools.partial(up_kernel, nx, ny, leaves),
         name="up",
         out_shape=(
             shape((leaves, 32, 128), f32),
-            shape((leaves, 64, 128), bf16),
-            shape((3, leaves // 2, 32, 128), bf16),
-            shape((32, 128), bf16),
+            shape((leaves, 32, 64), bf16),
             shape((8, 128), f32),
             shape((2 * HALO, 32, 128), bf16),
             shape((2, 7, HALO, 128), f32),
         ),
-        in_specs=[S, S, S] + [H] * 12,
-        out_specs=(H, H, H, V, V, H, H),
+        in_specs=[S] * 5 + [H] * 14,
+        out_specs=(H, H, V, H, H),
         scratch_shapes=[
             pltpu.VMEM((7, leaves, 128), f32),
             pltpu.VMEM((slots, 32, 128), bf16),
+            pltpu.VMEM((leaves, 64, 128), bf16),
             pltpu.VMEM((leaves, 64, 128), bf16),
             pltpu.VMEM((64, 64, leaves), bf16),
             pltpu.VMEM((64, 64, leaves), bf16),
@@ -643,12 +596,17 @@
             pltpu.VMEM((1, 64, 64), bf16),
             pltpu.VMEM(group_coupling.shape, bf16),
             pltpu.VMEM((2, 7, HALO, 128), f32),
+            pltpu.VMEM((2 * HALO, 32, 128), bf16),
             pltpu.VMEM((slots * SPITCH, 128), f32),
             pltpu.VMEM((leaves * TPITCH, 128), f32),
             pltpu.VMEM((slots, 128, 64), bf16),
             pltpu.VMEM((64 * RPITCH, 128), f32),
+            pltpu.VMEM(coupling.shape, bf16),
+            pltpu.VMEM((3, 64 * RPITCH, 128), f32),
             pltpu.VMEM((leaves, 64, 128), bf16),
-            pltpu.VMEM((leaves // 2, 32, 128), bf16),
+            pltpu.VMEM((3, leaves // 2, 32, 128), bf16),
+            pltpu.VMEM((3 * leaves + 1, 32, 128), bf16),
+            pltpu.VMEM((leaves, 32, 64), bf16),
             pltpu.VMEM((leaves // 2, 32, 256), bf16),
             pltpu.VMEM((3 * ny, 16, 128), bf16),
             pltpu.VMEM((ny, 16, 128), f32),
@@ -656,21 +614,34 @@
             pltpu.VMEM((nx // BRANCH, 64, 64), bf16),
             pltpu.VMEM((CHUNK, 8 * 128, 128), bf16),
             pltpu.VMEM((leaves, 32, 128), f32),
-            dma((12,)), dma((6,)), dma((4,)), dma((4,)), dma((2,)), dma((2,)), dma((3, ny)), dma((3 * ny,)),
+            dma((14,)), dma((6,)), dma((4,)), dma((4,)), dma((2,)), dma((2,)), dma((3, ny)), dma((3 * ny,)),
             dma((ny,)), dma((ny,)), dma((nx,)), dma((nx,)),
         ],
         compiler_params=pltpu.CompilerParams(
             collective_id=0, has_side_effects=True, vmem_limit_bytes=VMEM_LIMIT
         ),
     )(
-        ids, cluster_far, group_far, geo, densities, basis_in, up, down, cluster_up, cluster_down, cluster_coupling,
-        group_up, group_down, group_coupling, root_coupling,
+        ids, far, leaf_count, cluster_far, group_far, geo, densities, basis_in, up, down, cluster_up, cluster_down, cluster_coupling,
+        group_up, group_down, group_coupling, root_coupling, coupling, basis_out,
     )
     first = ((lax.axis_index("gx") * ny + lax.axis_index("gy")) * leaves).reshape(1)
-    return down_call(
-        leaves, first, extent, far, leaf_count, ids, mid, coupling, lift, coeff, near, basis_out, geo, geo_halo,
-        densities, dens_halo,
-    )
+    return pl.pallas_call(
+        functools.partial(finish_kernel, leaves),
+        name="finish",
+        out_shape=shape((leaves, 32, 128), f32),
+        in_specs=[S, V, S] + [H] * 7,
+        out_specs=H,
+        scratch_shapes=[
+            pltpu.VMEM((leaves, 32, 128), f32),
+            pltpu.VMEM((leaves, 32, 64), bf16),
+            pltpu.VMEM((leaves, 64, 128), bf16),
+            pltpu.VMEM((7, leaves, 128), f32),
+            pltpu.VMEM((2, 7, HALO, 128), f32),
+            pltpu.VMEM((slots, 32, 128), bf16),
+            dma((4,)), dma((4,)), dma((6,)),
+        ],
+        compiler_params=pltpu.CompilerParams(vmem_limit_bytes=VMEM_LIMIT),
+    )(first, extent, ids, total, field, basis_out, geo, geo_halo, densities, dens_halo)
 
 
 def solution(mesh):

time: 64.8 us -> 48.1 us (0.74)
  Pallas kernels: 64.7 us -> 47.9 us
    pallas_call x1, Pallas kernels: 15 us -> 3.11 us  [on_device(): pl.pallas_call(functools.partial(finish_kernel, leaves), name='finish', o...]
    pallas_call x1, Pallas kernels: 49.7 us -> 44.8 us  [on_device(): pl.pallas_call(functools.partial(up_kernel, nx, ny, leaves), name='up', o...]
where the time goes in v1:
time: 48.1 us; the launch traced here: 47.9 us
  Pallas kernels  47.9 us (100%)
    pallas_call x1, Pallas kernels, on_device(): pl.pallas_call(functools.partial(up_kernel, nx, ny, leaves), name='up', o...  44.8 us
    pallas_call x1, Pallas kernels, on_device(): pl.pallas_call(functools.partial(finish_kernel, leaves), name='finish', o...  3.11 us

profile of v1, /device:TPU:1, one launch (start us, length us, event | category | flops | bytes accessed | tf_op | source)
XLA Modules:
  0.0 47.9 jit_solution(1280498467839212267)
XLA Ops:
  0.0 44.8 %up.1 = (f32[96,32,128]{2,1,0:T(8,128)}, bf16[96,32,64]{2,1,0:T(8,128)(2,1)}, f32[8,128]{1,0:T(8,128)}, bf16[16,32,128]{2,1,0:T(8,128)(2,1)}, f32[2,7,8,128]{3,2,1,0:T(8,128)}) custom-call(s32[8,96]{1,0:T(8,128)} %bitcast.12, s32[6,96]{1,0:T(8,128)} %bitcast.14, s32[96]{0:T(128)} %count.1, s32[1,6]{1,0:T(1,128)} %cluster_far.1, s32[1,6]{1,0:T(1,128)} %group_far.1, ...), custom_call_target="tpu_custom_call" | custom-call | tf_op jit(solution)/shard_map/up/pallas_call | solution.py:573
  44.8 3.1 %finish.1 = f32[96,32,128]{2,1,0:T(8,128)} custom-call(s32[1]{0:T(128)} %bitcast.first_ref, f32[8,128]{1,0:T(8,128)} %get-tuple-element.10.extent, s32[8,96]{1,0:T(8,128)} %bitcast.13, f32[96,32,128]{2,1,0:T(8,128)} %get-tuple-element.11.total_hbm, bf16[96,32,64]{2,1,0:T(8,128)(2,1)} %get-tuple-element.12.field_hbm, bf16[96,64,128]{2,1,0:T(8,128)(2,1)} %basis_hbm.3, ...), custom_call_target="tpu_custom_call" | custom-call | tf_op jit(solution)/shard_map/finish/pallas_call | solution.py:628
